TPU v7x, 32 devices: a whole 2x2x4 slice. The times are simulated.
32 devices in a mesh: shard: 8 (over z, x), tensor: 4 (over y, core).
Axes of the slice: x: 2, y: 2, z: 4, core: 2. Of those that a mesh axis runs over, the one named last changes fastest.
Arguments:
- matrix_grads: bfloat16 [56, 512, 2560], P(None, 'shard', 'tensor'), may hold values from -64 to 64
- matrix_momentum: float32 [56, 512, 2560], P(None, 'shard', 'tensor'), may hold values from -64 to 64
- matrix_weights: float32 [56, 512, 2560], P(None, 'shard', 'tensor'), may hold values from -6 to 6
- table_grads: bfloat16 [2048, 2560], P('shard', 'tensor'), may hold values from -6 to 6
- table_state: float32 [3, 2048, 2560], P(None, 'shard', 'tensor'), may hold values from -4 to 4, as said below
- small_grads: bfloat16 [120, 2560], P(None, 'tensor'), may hold values from -6 to 6
- small_state: float32 [3, 120, 2560], P(None, None, 'tensor'), may hold values from -4 to 4, as said below
Outputs:
- matrix_update: float32 [56, 512, 2560], P(None, 'shard', 'tensor')
- momentum_next: float32 [56, 512, 2560], P(None, 'shard', 'tensor')
- table_out: float32 [2, 2048, 2560], P(None, 'shard', 'tensor')
- small_out: float32 [2, 120, 2560], P(None, None, 'tensor')
Inputs may be any that keep to these rules, and one draw needn't show every extreme that they name: `table_state`: index 0 holds weights, index 1 first moments, index 2 second moments, which lie between 0.0002 and 0.004. `small_state`: index 0 holds weights, index 1 first moments, index 2 second moments, which lie between 0.0002 and 0.004.
All inputs are finite; a program needn't handle non-finite values.
Results may differ from a plain program's by a relative error of at most 0.014.
The roundings to bfloat16 on the way count: a program that leaves them out, or rounds other values in their place, can miss the bound.
Values may be sent and summed in bfloat16 or wider, within the bound.
A program may use at most 192 MiB of HBM per device.

v0:
```python
import math
import jax
import jax.numpy as jnp
from jax import lax
from jax.sharding import PartitionSpec as P

D = 2560
KV = 512
EXPERTS = 64
ITERS = 5
COEF_A = 3.4445
COEF_B = -4.775
COEF_C = 2.0315
BIAS_ONE = 1.0 - 0.9**10
BIAS_TWO = 1.0 - 0.999**10


def unchanged(values):
    return values


def newton_schulz(blended, square_total, gram_total):
    squares = square_total(jnp.sum(jnp.square(blended.astype(jnp.float32)), axis=(1, 2)))
    iterate = (blended.astype(jnp.float32) / (jnp.sqrt(squares) + 1e-07)[:, None, None]).astype(
        jnp.bfloat16
    )
    iterate = lax.optimization_barrier(iterate)
    for turn in range(ITERS):
        gram_term = jnp.einsum("krc,ksc->krs", iterate, iterate, preferred_element_type=jnp.float32)
        gram_matrix = gram_total(gram_term).astype(jnp.bfloat16)
        gram_matrix = lax.optimization_barrier(gram_matrix)
        gram_square = jnp.einsum(
            "krs,kst->krt", gram_matrix, gram_matrix, preferred_element_type=jnp.float32
        )
        polynomial = (COEF_B * gram_matrix.astype(jnp.float32) + COEF_C * gram_square).astype(
            jnp.bfloat16
        )
        product = jnp.einsum(
            "krs,ksc->krc", polynomial, iterate, preferred_element_type=jnp.float32
        )
        iterate = (COEF_A * iterate.astype(jnp.float32) + product).astype(jnp.bfloat16)
        iterate = lax.optimization_barrier(iterate)
    return iterate


def pad_matrices(blended, total):
    extra = total - blended.shape[0]
    filler = jnp.zeros((extra,) + blended.shape[1:], blended.dtype)
    return jnp.concatenate([blended, filler], axis=0)


def adamw(gradient, states, decay_rate):
    grad_value = gradient.astype(jnp.float32)
    moment_one = 0.9 * states[1] + 0.1 * grad_value
    moment_two = 0.999 * states[2] + 0.001 * grad_value * grad_value
    direction = (
        moment_one / BIAS_ONE / (jnp.sqrt(moment_two / BIAS_TWO) + 1e-08) + decay_rate * states[0]
    )
    return jnp.stack([direction, moment_one])


def local(
    matrix_grads,
    matrix_momentum,
    matrix_weights,
    table_grads,
    table_state,
    small_grads,
    small_state,
):
    momentum_next = 0.95 * matrix_momentum + matrix_grads.astype(jnp.float32)
    blended = (matrix_grads.astype(jnp.float32) + 0.95 * momentum_next).astype(jnp.bfloat16)
    matrix_count, rows_local, cols_local = blended.shape
    shards = lax.axis_size("shard")
    tensor_size = lax.axis_size("tensor")
    devices = shards * tensor_size
    per_device = -(-matrix_count // devices)
    padded = pad_matrices(blended, per_device * devices)
    source = padded.reshape(shards, tensor_size, per_device, rows_local, cols_local)
    arrived = lax.all_to_all(
        lax.all_to_all(source, "shard", split_axis=0, concat_axis=3, tiled=True),
        "tensor",
        split_axis=1,
        concat_axis=4,
        tiled=True,
    )
    whole_result = newton_schulz(arrived[0, 0], unchanged, unchanged)
    returned = lax.all_to_all(
        lax.all_to_all(whole_result[None, None], "shard", split_axis=3, concat_axis=0, tiled=True),
        "tensor",
        split_axis=4,
        concat_axis=1,
        tiled=True,
    )
    orthogonal = returned.reshape(devices * per_device, rows_local, cols_local)[:matrix_count]
    muon_scale = 0.2 * math.sqrt(max(KV, D))
    matrix_update = muon_scale * orthogonal.astype(jnp.float32) + 0.1 * matrix_weights
    table_out = adamw(table_grads, table_state, 0.1)
    row_index = jnp.arange(small_grads.shape[0], dtype=jnp.int32)
    small_decay = jnp.where(row_index < EXPERTS, 0.1, 0.0).astype(jnp.float32)[:, None]
    small_out = adamw(small_grads, small_state, small_decay)
    return (matrix_update, momentum_next, table_out, small_out)


def solution(mesh):
    placed = (
        P(None, "shard", "tensor"),
        P(None, "shard", "tensor"),
        P(None, "shard", "tensor"),
        P("shard", "tensor"),
        P(None, "shard", "tensor"),
        P(None, "tensor"),
        P(None, None, "tensor"),
    )
    return jax.shard_map(
        local,
        mesh=mesh,
        in_specs=placed,
        out_specs=(
            P(None, "shard", "tensor"),
            P(None, "shard", "tensor"),
            P(None, "shard", "tensor"),
            P(None, None, "tensor"),
        ),
        check_vma=False,
    )
```

profile of v0, /device:TPU:0, one launch (start us, length us, event | category | flops | bytes accessed | tf_op | source)
XLA Modules:
  0.0 594.8 jit_solution(7325919482131494463)
XLA Ops:
  0.6 12.7 %fusion.1 = (bf16[56,64,640]{2,1,0:T(8,128)(2,1)}, f32[56,64,640]{2,1,0:T(8,128)}) fusion(bf16[56,64,640]{2,1,0:T(8,128)(2,1)} %param.7, f32[56,64,640]{2,1,0:T(8,128)} %param.8), kind=kLoop, calls=%fused_computation.11 | loop fusion | flops 13762560 | bytes 27525120 | tf_op jit(solution)/shard_map/convert_element_type | solution.py:72
  13.3 3.0 concatenate.3
  16.3 122.7 %all_to_all.60 = bf16[8,4,2,64,640]{4,3,2,1,0:T(8,128)(2,1)S(1)} all-to-all(bf16[8,4,2,64,640]{4,3,2,1,0:T(8,128)(2,1)S(1)} %bitcast.89), channel_id=1, replica_groups=mesh['shard'=8,'tensor'=4] {'shard'}, dimensions={0} | all-to-all | bytes 10485760 | tf_op jit(solution)/shard_map/all_to_all | solution.py:81
  139.6 62.5 %all_to_all.61 = bf16[1,4,2,512,640]{4,3,2,0,1:T(8,128)(2,1)S(1)} all-to-all(bf16[1,4,2,512,640]{4,3,2,0,1:T(8,128)(2,1)S(1)} %bitcast.90), channel_id=1, replica_groups=mesh['shard'=8,'tensor'=4] {'tensor'}, dimensions={1} | all-to-all | bytes 10485760 | tf_op jit(solution)/shard_map/all_to_all | solution.py:80
  202.1 1.5 fusion
  203.6 4.5 convert_bitcast_fusion
  208.2 14.7 %copy.35 = f32[1,1,2,512,4,640]{5,4,3,2,1,0:T(4,128)} copy(f32[1,1,2,512,4,640]{5,3,2,4,1,0:T(8,128)} %convert_bitcast_fusion) | data formatting | bytes 20971520 | tf_op jit(solution)/shard_map/convert_element_type | solution.py:24
  222.8 13.0 %reshape.44 = f32[2,512,2560]{2,1,0:T(8,128)} reshape(f32[1,1,2,512,4,640]{5,4,3,2,1,0:T(4,128)} %copy.35) | data formatting | bytes 20971520 | tf_op jit(solution)/shard_map/convert_element_type | solution.py:24
  235.8 5.3 divide_convert_fusion
  241.1 2.3 copy-done
  243.5 2.9 convolution_convert_fusion.4
  246.4 8.5 %add_convert_fusion.4 = bf16[2,512,2560]{2,1,0:T(8,128)(2,1)} fusion(bf16[2,512,2560]{2,1,0:T(8,128)(2,1)} %copy-done, bf16[2,512,512]{2,1,0:T(8,128)(2,1)S(1)} %convolution_convert_fusion.4), kind=kOutput, calls=%fused_computation.9 | convolution fusion | flops 3234332672 | bytes 11534336 | tf_op jit(solution)/shard_map/krs,ksc->krc/dot_general | solution.py:38
  254.9 6.9 %convolution_convert_fusion.3 = bf16[2,512,512]{2,1,0:T(8,128)(2,1)S(1)} fusion(bf16[2,512,2560]{2,1,0:T(8,128)(2,1)} %add_convert_fusion.4), kind=kOutput, calls=%fused_computation.22 | convolution fusion | flops 2684878848 | bytes 6291456 | tf_op jit(solution)/shard_map/krc,ksc->krs/dot_general | solution.py:29
  261.8 8.4 %add_convert_fusion.3 = bf16[2,512,2560]{2,1,0:T(8,128)(2,1)} fusion(bf16[2,512,2560]{2,1,0:T(8,128)(2,1)} %add_convert_fusion.4, bf16[2,512,512]{2,1,0:T(8,128)(2,1)S(1)} %convolution_convert_fusion.3), kind=kOutput, calls=%fused_computation.8 | convolution fusion | flops 3234332672 | bytes 11534336 | tf_op jit(solution)/shard_map/krs,ksc->krc/dot_general | solution.py:38
  270.2 6.9 %convolution_convert_fusion.2 = bf16[2,512,512]{2,1,0:T(8,128)(2,1)S(1)} fusion(bf16[2,512,2560]{2,1,0:T(8,128)(2,1)} %add_convert_fusion.3), kind=kOutput, calls=%fused_computation.21 | convolution fusion | flops 2684878848 | bytes 6291456 | tf_op jit(solution)/shard_map/krc,ksc->krs/dot_general | solution.py:29
  277.2 8.7 %add_convert_fusion.2 = bf16[2,512,2560]{2,1,0:T(8,128)(2,1)} fusion(bf16[2,512,2560]{2,1,0:T(8,128)(2,1)} %add_convert_fusion.3, bf16[2,512,512]{2,1,0:T(8,128)(2,1)S(1)} %convolution_convert_fusion.2), kind=kOutput, calls=%fused_computation.7 | convolution fusion | flops 3234332672 | bytes 11534336 | tf_op jit(solution)/shard_map/krs,ksc->krc/dot_general | solution.py:38
  285.9 6.9 %convolution_convert_fusion.1 = bf16[2,512,512]{2,1,0:T(8,128)(2,1)S(1)} fusion(bf16[2,512,2560]{2,1,0:T(8,128)(2,1)} %add_convert_fusion.2), kind=kOutput, calls=%fused_computation.20 | convolution fusion | flops 2684878848 | bytes 6291456 | tf_op jit(solution)/shard_map/krc,ksc->krs/dot_general | solution.py:29
  292.8 8.4 %add_convert_fusion.1 = bf16[2,512,2560]{2,1,0:T(8,128)(2,1)} fusion(bf16[2,512,2560]{2,1,0:T(8,128)(2,1)} %add_convert_fusion.2, bf16[2,512,512]{2,1,0:T(8,128)(2,1)S(1)} %convolution_convert_fusion.1), kind=kOutput, calls=%fused_computation.6 | convolution fusion | flops 3234332672 | bytes 11534336 | tf_op jit(solution)/shard_map/krs,ksc->krc/dot_general | solution.py:38
  301.3 6.9 %convolution_convert_fusion = bf16[2,512,512]{2,1,0:T(8,128)(2,1)S(1)} fusion(bf16[2,512,2560]{2,1,0:T(8,128)(2,1)} %add_convert_fusion.1), kind=kOutput, calls=%fused_computation.19 | convolution fusion | flops 2684878848 | bytes 6291456 | tf_op jit(solution)/shard_map/krc,ksc->krs/dot_general | solution.py:29
  308.2 8.7 %add_convert_fusion = bf16[2,512,2560]{2,1,0:T(8,128)(2,1)} fusion(bf16[2,512,2560]{2,1,0:T(8,128)(2,1)} %add_convert_fusion.1, bf16[2,512,512]{2,1,0:T(8,128)(2,1)S(1)} %convolution_convert_fusion), kind=kOutput, calls=%fused_computation.5 | convolution fusion | flops 3234332672 | bytes 11534336 | tf_op jit(solution)/shard_map/krs,ksc->krc/dot_general | solution.py:38
  316.9 10.2 %copy.36 = bf16[1,1,2,512,2560]{4,2,1,0,3:T(2,128)(2,1)} copy(bf16[1,1,2,512,2560]{4,3,2,1,0:T(8,128)(2,1)} %bitcast.93) | data formatting | bytes 10485760 | tf_op jit(solution)/shard_map/broadcast_in_dim | solution.py:89
  327.2 120.1 %all_to_all.62 = bf16[1,1,2,512,2560]{4,2,1,0,3:T(2,128)(2,1)} all-to-all(bf16[1,1,2,512,2560]{4,2,1,0,3:T(2,128)(2,1)} %copy.36), channel_id=1, replica_groups=mesh['shard'=8,'tensor'=4] {'shard'}, dimensions={3} | all-to-all | bytes 10485760 | tf_op jit(solution)/shard_map/all_to_all | solution.py:89
  447.3 17.4 %copy.37 = bf16[1,1,2,8,64,2560]{4,3,2,5,1,0:T(8,128)(2,1)} copy(bf16[1,1,2,8,64,2560]{5,2,4,3,1,0:T(2,128)(2,1)} %bitcast.91) | data formatting | bytes 10485760 | tf_op jit(solution)/shard_map/all_to_all | solution.py:89
  464.7 10.4 %bitcast_bitcast_fusion = bf16[2560,1,2,8,64]{4,3,2,1,0:T(8,128)(2,1)} fusion(bf16[1,1,2,8,64,2560]{4,3,2,5,1,0:T(8,128)(2,1)} %copy.37), kind=kLoop, calls=%fused_computation.61 | loop fusion | bytes 10485760
  475.0 11.2 %reshape.46 = bf16[4,2,327680]{2,1,0:T(2,128)(2,1)} reshape(bf16[2560,1,2,8,64]{4,3,2,1,0:T(8,128)(2,1)} %bitcast_bitcast_fusion) | data formatting | bytes 10485760
  486.2 5.6 all-to-all-start.3
  493.5 1.1 pad_maximum_fusion
  494.6 56.7 %all-to-all-done.3 = bf16[4,2,327680]{2,1,0:T(2,128)(2,1)} async-done(((bf16[4,2,327680]{2,1,0:T(2,128)(2,1)}), bf16[4,2,327680]{2,1,0:T(2,128)(2,1)}, u32[]{:S(2)}, u32[]{:S(2)}) %all-to-all-start.3) | async-done | bytes 5242912 | tf_op jit(solution)/shard_map/all_to_all | solution.py:88
  551.3 11.0 %reshape.47 = bf16[2560,1,2,8,64]{4,3,2,1,0:T(8,128)(2,1)} reshape(bf16[4,2,327680]{2,1,0:T(2,128)(2,1)} %all-to-all-done.3) | data formatting | bytes 10485760
  562.3 12.7 %copy.39 = bf16[8,1,2,64,4,640]{5,3,2,1,4,0:T(8,128)(2,1)} copy(bf16[8,1,2,64,4,640]{3,0,2,5,4,1:T(8,128)(2,1)} %bitcast.88) | data formatting | bytes 10485760 | tf_op jit(solution)/shard_map/all_to_all | solution.py:88
  575.0 7.1 %convert_multiply_fusion.1 = f32[7,4,1,2,64,640]{5,4,3,2,1,0:T(8,128)} fusion(bf16[8,4,1,2,64,640]{5,4,3,2,1,0:T(8,128)(2,1)} %bitcast.92), kind=kLoop, calls=%fused_computation.13 | loop fusion | flops 4587520 | bytes 13762560 | tf_op jit(solution)/shard_map/mul | solution.py:97
  582.1 12.4 %bitcast_add_fusion = f32[56,64,640]{2,1,0:T(8,128)} fusion(f32[7,4,1,2,64,640]{5,4,3,2,1,0:T(8,128)} %convert_multiply_fusion.1, f32[56,64,640]{2,1,0:T(8,128)} %param.9), kind=kLoop, calls=%fused_computation.12 | loop fusion | flops 4587520 | bytes 27525120 | tf_op jit(solution)/shard_map/add | solution.py:97
  (15 shorter events, 2.2 us)
Async XLA Ops:
  241.1 2.4 copy-start
  486.2 5.7 copy-start.2
  486.2 5.7 copy-start.4
  486.2 6.8 %copy-start.1 = (f32[3,256,640]{2,1,0:T(8,128)S(1)}, f32[3,256,640]{2,1,0:T(8,128)}, u32[]{:S(2)}) copy-start(f32[3,256,640]{2,1,0:T(8,128)} %param.11) | copy-start | bytes 5898244
  486.2 6.8 %copy-start.3 = (bf16[256,640]{1,0:T(8,128)(2,1)S(1)}, bf16[256,640]{1,0:T(8,128)(2,1)}, u32[]{:S(2)}) copy-start(bf16[256,640]{1,0:T(8,128)(2,1)} %param.10) | copy-start | bytes 983044
  486.2 65.1 %all-to-all-start.3 = ((bf16[4,2,327680]{2,1,0:T(2,128)(2,1)}), bf16[4,2,327680]{2,1,0:T(2,128)(2,1)}, u32[]{:S(2)}, u32[]{:S(2)}) async-start(bf16[4,2,327680]{2,1,0:T(2,128)(2,1)} %reshape.46), calls=%async_computation.3 | async-start | bytes 10485760 | tf_op jit(solution)/shard_map/all_to_all | solution.py:88
where the time goes:
time: 599 us; the launch traced here: 595 us
  blocking collectives  305 us (51%)
  local copies, waits for them, and re-layouts  106 us (18%)
  matrix products  73.4 us (12%)
  waiting for transfers between devices  56.7 us (9%)
  other arithmetic  46.2 us (8%)
    all_to_all x1, blocking collectives, local(): lax.all_to_all(source, 'shard', split_axis=0, concat_axis=3, tiled=True)  123 us
    all_to_all x1, blocking collectives, local(): lax.all_to_all(whole_result[None, None], 'shard', split_axis=3, concat_ax...  120 us
    all_to_all x1, blocking collectives, local(): lax.all_to_all(lax.all_to_all(source, 'shard', split_axis=0, concat_axis=...  62.5 us
    all_to_all x1, waiting for transfers between devices, local(): lax.all_to_all(lax.all_to_all(whole_result[None, None], 'shard', split_ax...  56.7 us
    dot_general x5, matrix products, newton_schulz(): jnp.einsum('krs,ksc->krc', polynomial, iterate, preferred_element_type=jn...  42.7 us
    unnamed x13, local copies, waits for them, and re-layouts  34.9 us
    dot_general x5, matrix products, newton_schulz(): jnp.einsum('krc,ksc->krs', iterate, iterate, preferred_element_type=jnp.f...  30.7 us
    convert_element_type x2, local copies, waits for them, and re-layouts, newton_schulz(): blended.astype(jnp.float32) / (jnp.sqrt(squares) + 1e-07)[:, None, None]  27.6 us
  transfers between devices with their start and end apart: 1, of which 1 were waited for; matrix products, arithmetic and copies ran while one was open for 0% of the time, Pallas kernels for 0%

commit v1 on v0

--- a/solution.py
+++ b/solution.py
@@ -13,6 +13,22 @@
 COEF_C = 2.0315
 BIAS_ONE = 1.0 - 0.9**10
 BIAS_TWO = 1.0 - 0.999**10
+
+
+def pairwise_exchange(x, axis, split, join):
+    ways, here = (lax.axis_size(axis), lax.axis_index(axis))
+    width = x.shape[split] // ways
+    shape = list(x.shape)
+    shape[split] = width
+    height = shape[join]
+    shape[join] = height * ways
+    full = jnp.zeros(shape, x.dtype)
+    for mask in range(ways):
+        part = lax.dynamic_slice_in_dim(x, (here ^ mask) * width, width, axis=split)
+        if mask:
+            part = lax.ppermute(part, axis, [(d, d ^ mask) for d in range(ways)])
+        full = lax.dynamic_update_slice_in_dim(full, part, (here ^ mask) * height, axis=join)
+    return full
 
 
 def unchanged(values):
@@ -77,12 +93,8 @@
     per_device = -(-matrix_count // devices)
     padded = pad_matrices(blended, per_device * devices)
     source = padded.reshape(shards, tensor_size, per_device, rows_local, cols_local)
-    arrived = lax.all_to_all(
-        lax.all_to_all(source, "shard", split_axis=0, concat_axis=3, tiled=True),
-        "tensor",
-        split_axis=1,
-        concat_axis=4,
-        tiled=True,
+    arrived = pairwise_exchange(
+        lax.all_to_all(source, "shard", split_axis=0, concat_axis=3, tiled=True), "tensor", 1, 4
     )
     whole_result = newton_schulz(arrived[0, 0], unchanged, unchanged)
     returned = lax.all_to_all(

time: 599 us -> 570 us (0.952)
  blocking collectives: 305 us -> 121 us
  waiting for transfers between devices: 56.7 us -> 226 us
  local copies, waits for them, and re-layouts: 106 us -> 92 us
  starting transfers between devices: 5.62 us -> 15 us
  other arithmetic: 46.2 us -> 37.5 us
    all_to_all x2 -> x0, blocking collectives: 185 us -> none  [the longest x1 123 us: local(): lax.all_to_all(source, 'shard', split_axis=0, concat_axis=3, tiled=True)]
    all_to_all x0 -> x1, waiting for transfers between devices: none -> 116 us  [local(): lax.all_to_all(source, 'shard', split_axis=0, concat_axis=3, tiled=True)]
    ppermute x0 -> x3, waiting for transfers between devices: none -> 53.6 us  [pairwise_exchange(): part = lax.ppermute(part, axis, [(d, d ^ mask) for d in range(ways)])]
    convert_element_type x2 -> x0, local copies, waits for them, and re-layouts: 27.6 us -> none  [newton_schulz(): blended.astype(jnp.float32) / (jnp.sqrt(squares) + 1e-07)[:, None, None]]
    all_to_all x0 -> x1, starting transfers between devices: none -> 7.6 us  [local(): lax.all_to_all(source, 'shard', split_axis=0, concat_axis=3, tiled=True)]
    unnamed x13 -> x15, local copies, waits for them, and re-layouts: 34.9 us -> 37.3 us
  transfers between devices with their start and end apart: 1 -> 5, of which waited for: 1 -> 4; matrix products, arithmetic and copies ran while one was open for 0% -> 1% of each run, Pallas kernels for 0% -> 0%
where the time goes in v1:
time: 570 us; the launch traced here: 566 us
  waiting for transfers between devices  226 us (40%)
  blocking collectives  121 us (21%)
  local copies, waits for them, and re-layouts  92 us (16%)
  matrix products  73.5 us (13%)
  other arithmetic  37.5 us (7%)
  starting transfers between devices  15 us (3%)
    all_to_all x1, blocking collectives, local(): lax.all_to_all(whole_result[None, None], 'shard', split_axis=3, concat_ax...  121 us
    all_to_all x1, waiting for transfers between devices, local(): lax.all_to_all(source, 'shard', split_axis=0, concat_axis=3, tiled=True)  116 us
    all_to_all x1, waiting for transfers between devices, local(): lax.all_to_all(lax.all_to_all(whole_result[None, None], 'shard', split_ax...  56.7 us
    ppermute x3, waiting for transfers between devices, pairwise_exchange(): part = lax.ppermute(part, axis, [(d, d ^ mask) for d in range(ways)])  53.6 us
    dot_general x5, matrix products, newton_schulz(): jnp.einsum('krs,ksc->krc', polynomial, iterate, preferred_element_type=jn...  42.8 us
    unnamed x15, local copies, waits for them, and re-layouts  37.3 us
    dot_general x5, matrix products, newton_schulz(): jnp.einsum('krc,ksc->krs', iterate, iterate, preferred_element_type=jnp.f...  30.7 us
    all_to_all x1, local copies, waits for them, and re-layouts, local(): lax.all_to_all(whole_result[None, None], 'shard', split_axis=3, concat_ax...  17.4 us
  transfers between devices with their start and end apart: 5, of which 4 were waited for; matrix products, arithmetic and copies ran while one was open for 1% of the time, Pallas kernels for 0%

profile of v1, /device:TPU:0, one launch (start us, length us, event | category | flops | bytes accessed | tf_op | source)
XLA Modules:
  0.0 565.7 jit_solution(7635064692515404357)
XLA Ops:
  0.6 12.7 %fusion.2 = (bf16[56,64,640]{2,1,0:T(8,128)(2,1)}, f32[56,64,640]{2,1,0:T(8,128)}) fusion(bf16[56,64,640]{2,1,0:T(8,128)(2,1)} %param.7, f32[56,64,640]{2,1,0:T(8,128)} %param.8), kind=kLoop, calls=%fused_computation.11 | loop fusion | flops 13762560 | bytes 27525120 | tf_op jit(solution)/shard_map/convert_element_type | solution.py:88
  13.3 5.3 concatenate.3
  18.6 7.6 %all-to-all-start = ((bf16[8,4,2,64,640]{4,3,2,1,0:T(8,128)(2,1)}), bf16[8,4,2,64,640]{4,3,2,1,0:T(8,128)(2,1)}, u32[]{:S(2)}, u32[]{:S(2)}) async-start(bf16[8,4,2,64,640]{4,3,2,1,0:T(8,128)(2,1)} %bitcast.92), calls=%async_computation | async-start | bytes 10485760 | tf_op jit(solution)/shard_map/all_to_all | solution.py:97
  26.2 115.7 %all-to-all-done = bf16[8,4,2,64,640]{4,3,2,1,0:T(8,128)(2,1)} async-done(((bf16[8,4,2,64,640]{4,3,2,1,0:T(8,128)(2,1)}), bf16[8,4,2,64,640]{4,3,2,1,0:T(8,128)(2,1)}, u32[]{:S(2)}, u32[]{:S(2)}) %all-to-all-start) | async-done | bytes 5242912 | tf_op jit(solution)/shard_map/all_to_all | solution.py:97
  141.9 3.1 copy.20
  145.0 2.3 copy-done
  147.4 2.0 constant_dynamic-slice_fusion
  151.6 1.5 bitcast_dynamic-update-slice_fusion.3
  154.7 26.5 %collective-permute-done.1 = bf16[1,1,2,512,640]{4,3,2,1,0:T(8,128)(2,1)S(1)} collective-permute-done((bf16[1,1,2,512,640]{4,3,2,1,0:T(8,128)(2,1)}, bf16[1,1,2,512,640]{4,3,2,1,0:T(8,128)(2,1)S(1)}, u32[]{:S(2)}, u32[]{:S(2)}) %collective-permute-start.1) | collective-permute-done | bytes 1310752 | tf_op jit(solution)/shard_map/ppermute | solution.py:29
  181.4 27.1 %collective-permute-done.2 = bf16[1,1,2,512,640]{4,3,2,1,0:T(8,128)(2,1)S(1)} collective-permute-done((bf16[1,1,2,512,640]{4,3,2,1,0:T(8,128)(2,1)}, bf16[1,1,2,512,640]{4,3,2,1,0:T(8,128)(2,1)S(1)}, u32[]{:S(2)}, u32[]{:S(2)}) %collective-permute-start.2) | collective-permute-done | bytes 1310752 | tf_op jit(solution)/shard_map/ppermute | solution.py:29
  211.4 2.3 copy-done.1
  213.7 2.9 convolution_convert_fusion.4
  216.6 8.4 %add_convert_fusion.4 = bf16[2,512,2560]{2,1,0:T(8,128)(2,1)} fusion(bf16[2,512,2560]{2,1,0:T(8,128)(2,1)} %copy-done.1, bf16[2,512,512]{2,1,0:T(8,128)(2,1)S(1)} %convolution_convert_fusion.4), kind=kOutput, calls=%fused_computation.10 | convolution fusion | flops 3234332672 | bytes 11534336 | tf_op jit(solution)/shard_map/krs,ksc->krc/dot_general | solution.py:54
  225.0 6.9 %convolution_convert_fusion.3 = bf16[2,512,512]{2,1,0:T(8,128)(2,1)S(1)} fusion(bf16[2,512,2560]{2,1,0:T(8,128)(2,1)} %add_convert_fusion.4), kind=kOutput, calls=%fused_computation.22 | convolution fusion | flops 2684878848 | bytes 6291456 | tf_op jit(solution)/shard_map/krc,ksc->krs/dot_general | solution.py:45
  232.0 8.9 %add_convert_fusion.3 = bf16[2,512,2560]{2,1,0:T(8,128)(2,1)} fusion(bf16[2,512,2560]{2,1,0:T(8,128)(2,1)} %add_convert_fusion.4, bf16[2,512,512]{2,1,0:T(8,128)(2,1)S(1)} %convolution_convert_fusion.3), kind=kOutput, calls=%fused_computation.9 | convolution fusion | flops 3234332672 | bytes 11534336 | tf_op jit(solution)/shard_map/krs,ksc->krc/dot_general | solution.py:54
  240.9 7.0 %convolution_convert_fusion.2 = bf16[2,512,512]{2,1,0:T(8,128)(2,1)S(1)} fusion(bf16[2,512,2560]{2,1,0:T(8,128)(2,1)} %add_convert_fusion.3), kind=kOutput, calls=%fused_computation.21 | convolution fusion | flops 2684878848 | bytes 6291456 | tf_op jit(solution)/shard_map/krc,ksc->krs/dot_general | solution.py:45
  247.9 8.4 %add_convert_fusion.2 = bf16[2,512,2560]{2,1,0:T(8,128)(2,1)} fusion(bf16[2,512,2560]{2,1,0:T(8,128)(2,1)} %add_convert_fusion.3, bf16[2,512,512]{2,1,0:T(8,128)(2,1)S(1)} %convolution_convert_fusion.2), kind=kOutput, calls=%fused_computation.8 | convolution fusion | flops 3234332672 | bytes 11534336 | tf_op jit(solution)/shard_map/krs,ksc->krc/dot_general | solution.py:54
  256.3 6.9 %convolution_convert_fusion.1 = bf16[2,512,512]{2,1,0:T(8,128)(2,1)S(1)} fusion(bf16[2,512,2560]{2,1,0:T(8,128)(2,1)} %add_convert_fusion.2), kind=kOutput, calls=%fused_computation.20 | convolution fusion | flops 2684878848 | bytes 6291456 | tf_op jit(solution)/shard_map/krc,ksc->krs/dot_general | solution.py:45
  263.3 8.4 %add_convert_fusion.1 = bf16[2,512,2560]{2,1,0:T(8,128)(2,1)} fusion(bf16[2,512,2560]{2,1,0:T(8,128)(2,1)} %add_convert_fusion.2, bf16[2,512,512]{2,1,0:T(8,128)(2,1)S(1)} %convolution_convert_fusion.1), kind=kOutput, calls=%fused_computation.7 | convolution fusion | flops 3234332672 | bytes 11534336 | tf_op jit(solution)/shard_map/krs,ksc->krc/dot_general | solution.py:54
  271.7 6.9 %convolution_convert_fusion = bf16[2,512,512]{2,1,0:T(8,128)(2,1)S(1)} fusion(bf16[2,512,2560]{2,1,0:T(8,128)(2,1)} %add_convert_fusion.1), kind=kOutput, calls=%fused_computation.19 | convolution fusion | flops 2684878848 | bytes 6291456 | tf_op jit(solution)/shard_map/krc,ksc->krs/dot_general | solution.py:45
  278.7 8.6 %add_convert_fusion = bf16[2,512,2560]{2,1,0:T(8,128)(2,1)} fusion(bf16[2,512,2560]{2,1,0:T(8,128)(2,1)} %add_convert_fusion.1, bf16[2,512,512]{2,1,0:T(8,128)(2,1)S(1)} %convolution_convert_fusion), kind=kOutput, calls=%fused_computation.6 | convolution fusion | flops 3234332672 | bytes 11534336 | tf_op jit(solution)/shard_map/krs,ksc->krc/dot_general | solution.py:54
  287.2 10.2 %copy.21 = bf16[1,1,2,512,2560]{4,2,1,0,3:T(2,128)(2,1)} copy(bf16[1,1,2,512,2560]{4,3,2,1,0:T(8,128)(2,1)} %bitcast.95) | data formatting | bytes 10485760 | tf_op jit(solution)/shard_map/broadcast_in_dim | solution.py:101
  297.5 120.8 %all_to_all.51 = bf16[1,1,2,512,2560]{4,2,1,0,3:T(2,128)(2,1)} all-to-all(bf16[1,1,2,512,2560]{4,2,1,0,3:T(2,128)(2,1)} %copy.21), channel_id=1, replica_groups=mesh['shard'=8,'tensor'=4] {'shard'}, dimensions={3} | all-to-all | bytes 10485760 | tf_op jit(solution)/shard_map/all_to_all | solution.py:101
  418.3 17.4 %copy.22 = bf16[1,1,2,8,64,2560]{4,3,2,5,1,0:T(8,128)(2,1)} copy(bf16[1,1,2,8,64,2560]{5,2,4,3,1,0:T(2,128)(2,1)} %bitcast.93) | data formatting | bytes 10485760 | tf_op jit(solution)/shard_map/all_to_all | solution.py:101
  435.7 10.4 %bitcast_bitcast_fusion = bf16[2560,1,2,8,64]{4,3,2,1,0:T(8,128)(2,1)} fusion(bf16[1,1,2,8,64,2560]{4,3,2,5,1,0:T(8,128)(2,1)} %copy.22), kind=kLoop, calls=%fused_computation.68 | loop fusion | bytes 10485760
  446.1 11.2 %reshape.45 = bf16[4,2,327680]{2,1,0:T(2,128)(2,1)} reshape(bf16[2560,1,2,8,64]{4,3,2,1,0:T(8,128)(2,1)} %bitcast_bitcast_fusion) | data formatting | bytes 10485760
  457.3 5.5 all-to-all-start.2
  465.6 56.7 %all-to-all-done.2 = bf16[4,2,327680]{2,1,0:T(2,128)(2,1)} async-done(((bf16[4,2,327680]{2,1,0:T(2,128)(2,1)}), bf16[4,2,327680]{2,1,0:T(2,128)(2,1)}, u32[]{:S(2)}, u32[]{:S(2)}) %all-to-all-start.2) | async-done | bytes 5242912 | tf_op jit(solution)/shard_map/all_to_all | solution.py:100
  522.3 11.0 %reshape.46 = bf16[2560,1,2,8,64]{4,3,2,1,0:T(8,128)(2,1)} reshape(bf16[4,2,327680]{2,1,0:T(2,128)(2,1)} %all-to-all-done.2) | data formatting | bytes 10485760
  533.3 12.7 %copy.24 = bf16[8,1,2,64,4,640]{5,3,2,1,4,0:T(8,128)(2,1)} copy(bf16[8,1,2,64,4,640]{3,0,2,5,4,1:T(8,128)(2,1)} %bitcast.89) | data formatting | bytes 10485760 | tf_op jit(solution)/shard_map/all_to_all | solution.py:100
  546.0 7.1 %convert_multiply_fusion.1 = f32[7,4,1,2,64,640]{5,4,3,2,1,0:T(8,128)} fusion(bf16[8,4,1,2,64,640]{5,4,3,2,1,0:T(8,128)(2,1)} %bitcast.94), kind=kLoop, calls=%fused_computation.13 | loop fusion | flops 4587520 | bytes 13762560 | tf_op jit(solution)/shard_map/mul | solution.py:109
  553.1 12.4 %bitcast_add_fusion = f32[56,64,640]{2,1,0:T(8,128)} fusion(f32[7,4,1,2,64,640]{5,4,3,2,1,0:T(8,128)} %convert_multiply_fusion.1, f32[56,64,640]{2,1,0:T(8,128)} %param.9), kind=kLoop, calls=%fused_computation.12 | loop fusion | flops 4587520 | bytes 27525120 | tf_op jit(solution)/shard_map/add | solution.py:109
  (26 shorter events, 9.6 us)
Async XLA Ops:
  18.6 123.3 %all-to-all-start = ((bf16[8,4,2,64,640]{4,3,2,1,0:T(8,128)(2,1)}), bf16[8,4,2,64,640]{4,3,2,1,0:T(8,128)(2,1)}, u32[]{:S(2)}, u32[]{:S(2)}) async-start(bf16[8,4,2,64,640]{4,3,2,1,0:T(8,128)(2,1)} %bitcast.92), calls=%async_computation | async-start | bytes 10485760 | tf_op jit(solution)/shard_map/all_to_all | solution.py:97
  145.0 2.4 copy-start
  149.4 3.8 collective-permute-start
  149.4 31.8 %collective-permute-start.1 = (bf16[1,1,2,512,640]{4,3,2,1,0:T(8,128)(2,1)}, bf16[1,1,2,512,640]{4,3,2,1,0:T(8,128)(2,1)S(1)}, u32[]{:S(2)}, u32[]{:S(2)}) collective-permute-start(bf16[1,1,2,512,640]{4,3,2,1,0:T(8,128)(2,1)} %get-tuple-element.7), channel_id=1, source_target_pairs={{0,2},{1,3},{2,0},{3,1},{4,6},{5,7},{6,4},{7,5},{8,10},{9,11},{10,... | collective-permute-start | bytes 3932168 | tf_op jit(solution)/shard_map/ppermute | solution.py:29
  150.9 57.6 %collective-permute-start.2 = (bf16[1,1,2,512,640]{4,3,2,1,0:T(8,128)(2,1)}, bf16[1,1,2,512,640]{4,3,2,1,0:T(8,128)(2,1)S(1)}, u32[]{:S(2)}, u32[]{:S(2)}) collective-permute-start(bf16[1,1,2,512,640]{4,3,2,1,0:T(8,128)(2,1)} %get-tuple-element.6), channel_id=1, source_target_pairs={{0,3},{1,2},{2,1},{3,0},{4,7},{5,6},{6,5},{7,4},{8,11},{9,10},{10,... | collective-permute-start | bytes 3932168 | tf_op jit(solution)/shard_map/ppermute | solution.py:29
  211.4 2.4 copy-start.1
  457.2 5.6 copy-start.3
  457.2 5.6 copy-start.5
  457.2 6.7 %copy-start.2 = (f32[3,256,640]{2,1,0:T(8,128)S(1)}, f32[3,256,640]{2,1,0:T(8,128)}, u32[]{:S(2)}) copy-start(f32[3,256,640]{2,1,0:T(8,128)} %param.11) | copy-start | bytes 5898244
  457.2 6.7 %copy-start.4 = (bf16[256,640]{1,0:T(8,128)(2,1)S(1)}, bf16[256,640]{1,0:T(8,128)(2,1)}, u32[]{:S(2)}) copy-start(bf16[256,640]{1,0:T(8,128)(2,1)} %param.10) | copy-start | bytes 983044
  457.3 65.0 %all-to-all-start.2 = ((bf16[4,2,327680]{2,1,0:T(2,128)(2,1)}), bf16[4,2,327680]{2,1,0:T(2,128)(2,1)}, u32[]{:S(2)}, u32[]{:S(2)}) async-start(bf16[4,2,327680]{2,1,0:T(2,128)(2,1)} %reshape.45), calls=%async_computation.2 | async-start | bytes 10485760 | tf_op jit(solution)/shard_map/all_to_all | solution.py:100
